TPU v7x, 32 devices: a whole 2x2x4 slice. The times are simulated.
32 devices in a mesh: row: 8 (over z, y), col: 4 (over x, core).
Axes of the slice: x: 2, y: 2, z: 4, core: 2. Of those that a mesh axis runs over, the one named last changes fastest.
Arguments:
- query_acts: bfloat16 [256, 8192], P('col', 'row'), may hold values from -6 to 6
- query_grads: bfloat16 [256, 28672], P('row', 'col'), may hold values from -6 to 6
- ritz_mats: float32 [3, 8192, 28672], P(None, 'row', 'col'), may hold values from -0.095683193 to 0.095683193, as said below
- eigenvalues: float32 [3], replicated, may hold values from 0.5 to 4
- train_acts: bfloat16 [64, 8192], P('row'), may hold values from -6 to 6
- train_grads: bfloat16 [64, 28672], P('row', 'col'), may hold values from -6 to 6
Outputs:
- response: bfloat16 [64, 28672], P('row', 'col')
- scores: float32 [64], P('row')
Inputs may be any that keep to these rules, and one draw needn't show every extreme that they name: `ritz_mats`: real entries of order one over the square root of 8192; every matrix has full rank.
All inputs are finite; a program needn't handle non-finite values.
Results may differ from a plain program's by a relative error of at most 0.0012.
Values may be sent and summed in bfloat16 or wider, within the bound.
No kernel may reach another device: no remote copies, remote signals or barrier semaphores. Data moves between devices by JAX's collectives and lax.ppermute only.
A program may use at most 192 MiB of HBM per device.

v0:
```python
import math
import jax
import jax.numpy as jnp
from jax import lax
from jax.sharding import PartitionSpec as P

D_OUT = 28672
QUERY = 256
highest = lax.Precision.HIGHEST


def per_device(query_acts, query_grads, ritz_mats, eigenvalues, train_acts, train_grads):
    outer_cols = ritz_mats.shape[2]
    acts_all = lax.all_gather(query_acts, "col", axis=0, tiled=True)
    grad_tile = lax.dot_general(
        acts_all,
        lax.all_gather(query_grads, "row", axis=0, tiled=True),
        (((0,), (0,)), ((), ())),
        preferred_element_type=jnp.float32,
    )
    local_terms = jnp.sum(ritz_mats * grad_tile[None], axis=(1, 2))
    coeffs = lax.psum(local_terms, ("row", "col"))
    weights = coeffs / (eigenvalues * math.sqrt(QUERY * D_OUT))
    train_local = lax.all_to_all(train_acts, "row", split_axis=1, concat_axis=0, tiled=True).astype(
        jnp.float32
    )
    root_width = math.sqrt(D_OUT)
    total = jnp.zeros((lax.axis_size("row") * train_acts.shape[0], outer_cols), jnp.float32)
    for which in range(ritz_mats.shape[0]):
        total = total + weights[which] * jnp.dot(train_local, ritz_mats[which], precision=highest)
    response_full = lax.psum_scatter(total, "row", scatter_dimension=0, tiled=True)
    score_terms = jnp.sum(response_full * train_grads.astype(jnp.float32), axis=1) / root_width
    scores = lax.psum(score_terms, "col")
    response = response_full.astype(jnp.bfloat16)
    return (response, scores)


def solution(mesh):
    in_specs = (
        P("col", "row"),
        P("row", "col"),
        P(None, "row", "col"),
        P(),
        P("row", None),
        P("row", "col"),
    )
    out_specs = (P("row", "col"), P("row"))
    return jax.shard_map(
        per_device, mesh=mesh, in_specs=in_specs, out_specs=out_specs, check_vma=False
    )
```

profile of v0, /device:TPU:0, one launch (start us, length us, event | category | flops | bytes accessed | tf_op | source)
XLA Modules:
  0.0 306.3 jit_solution(11983988093099938950)
XLA Ops:
  7.2 0.0 all-gather.2.cloned.1.call-start
  7.2 0.7 all-gather.2.cloned.1.call-update
  7.9 8.9 %all_gather.6 = bf16[256,1024]{1,0:T(8,128)(2,1)S(1)} all-gather(bf16[64,1024]{1,0:T(8,128)(2,1)} %param.6), channel_id=1, replica_groups=mesh['row'=8,'col'=4] {'col'}, dimensions={0}, use_global_device_ids=true | all-gather | bytes 655360 | tf_op jit(solution)/shard_map/all_gather | solution.py:14
  16.8 62.4 %all-gather.2.cloned.1.call-done = bf16[256,7168]{1,0:T(8,128)(2,1)} async-done(((bf16[32,7168]{1,0:T(8,128)(2,1)}), bf16[256,7168]{1,0:T(8,128)(2,1)}) %all-gather.2.cloned.1.call-update) | async-done | bytes 3670032 | tf_op jit(solution)/shard_map/all_gather | solution.py:17
  79.1 13.7 %fusion.28 = f32[1024,7168]{1,0:T(8,128)} fusion(bf16[256,1024]{1,0:T(8,128)(2,1)S(1)} %all_gather.6, bf16[256,7168]{1,0:T(8,128)(2,1)} %all-gather.2.cloned.1.call-done), kind=kOutput, calls=%fused_computation.22 | convolution fusion | flops 3758096384 | bytes 33554432 | tf_op jit(solution)/shard_map/dot_general | solution.py:15
  92.8 0.0 copy-start.1
  92.8 35.5 %multiply_reduce_fusion = f32[3]{0:T(128)S(1)} fusion(f32[3,1024,7168]{2,1,0:T(8,128)} %param.8, f32[1024,7168]{1,0:T(8,128)} %fusion.28), kind=kLoop, calls=%fused_computation | loop fusion | flops 44040188 | bytes 117440528 | tf_op jit(solution)/shard_map/reduce_sum | solution.py:21
  128.4 3.4 %all-to-all-start = ((bf16[8,8,1024]{2,0,1:T(8,128)(2,1)}), bf16[8,8,1024]{2,0,1:T(8,128)(2,1)S(1)}, u32[]{:S(2)}, u32[]{:S(2)}) async-start(bf16[8,8,1024]{2,0,1:T(8,128)(2,1)} %bitcast.1), calls=%async_computation | async-start | bytes 262144 | tf_op jit(solution)/shard_map/all_to_all | solution.py:24
  131.8 0.0 reduce-scatter.2.cloned.1.call-start
  131.8 40.7 %psum.14 = f32[3]{0:T(128)S(1)} all-reduce(f32[3]{0:T(128)S(1)} %multiply_reduce_fusion), channel_id=1, replica_groups=mesh['row'=8,'col'=4] {'row','col'}, use_global_device_ids=true, to_apply=%region_1.0 | all-reduce | flops 3 | bytes 24 | tf_op jit(solution)/shard_map/psum | solution.py:22
  172.5 0.0 copy-done.1
  172.5 0.7 fusion.27
  173.2 0.0 all-to-all-done
  173.2 15.6 %fusion.15 = f32[64,7168]{1,0:T(8,128)S(1)} fusion(f32[3,1024,7168]{2,1,0:T(8,128)} %param.8, f32[]{:T(128)} %bitcast.5, bf16[8,8,1024]{2,0,1:T(8,128)(2,1)S(1)} %all-to-all-done), kind=kOutput, calls=%fused_computation.12 | convolution fusion | flops 5637603328 | bytes 31326720 | tf_op jit(solution)/shard_map/dot_general | solution.py:30
  188.8 18.0 %fusion.12 = f32[64,7168]{1,0:T(8,128)S(1)} fusion(f32[64,7168]{1,0:T(8,128)S(1)} %fusion.15, f32[3,1024,7168]{2,1,0:T(8,128)} %param.8, f32[]{:T(128)} %bitcast, bf16[8,8,1024]{2,0,1:T(8,128)(2,1)S(1)} %all-to-all-done), kind=kOutput, calls=%fused_computation.11 | convolution fusion | flops 5638062080 | bytes 33161728 | tf_op jit(solution)/shard_map/dot_general | solution.py:30
  206.8 0.0 copy-start
  206.8 17.5 %fusion.21 = f32[64,7168]{1,0:T(8,128)} fusion(f32[64,7168]{1,0:T(8,128)S(1)} %fusion.12, f32[3,1024,7168]{2,1,0:T(8,128)} %param.8, f32[]{:T(128)} %bitcast.8, bf16[8,8,1024]{2,0,1:T(8,128)(2,1)S(1)} %all-to-all-done), kind=kOutput, calls=%fused_computation.14 | convolution fusion | flops 5638062080 | bytes 33161728 | tf_op jit(solution)/shard_map/dot_general | solution.py:30
  224.3 0.0 reduce-scatter.2.cloned.1.call-update
  224.3 67.2 %reduce-scatter.2.cloned.1.call-done = f32[8,7168]{1,0:T(8,128)} async-done(((f32[64,7168]{1,0:T(8,128)}), f32[8,7168]{1,0:T(8,128)}) %reduce-scatter.2.cloned.1.call-update) | async-done | bytes 229392 | tf_op jit(solution)/shard_map/reduce_scatter | solution.py:31
  291.5 0.0 copy-done
  291.5 1.8 multiply_reduce_fusion.1
  293.3 6.2 %psum.15 = f32[8]{0:T(128)} all-reduce(f32[8]{0:T(128)S(1)} %broadcast_multiply_fusion), channel_id=1, replica_groups=mesh['row'=8,'col'=4] {'col'}, use_global_device_ids=true, to_apply=%region_4.0 | all-reduce | flops 8 | bytes 64 | tf_op jit(solution)/shard_map/psum | solution.py:33
  (2 shorter events, 0.0 us)
Async XLA Ops:
  7.2 72.0 %all-gather.2.cloned.1.call-start = ((), (), s32[]{:S(2)}) async-start(), calls=%async_computation.2 | async-start | bytes 4128768 | tf_op jit(solution)/shard_map/all_gather | solution.py:17
  92.8 79.7 %copy-start.1 = (f32[3]{0:T(128)S(1)}, f32[3]{0:T(128)}, u32[]{:S(2)}) copy-start(f32[3]{0:T(128)} %param.9) | copy-start | bytes 40
  128.4 44.8 %all-to-all-start = ((bf16[8,8,1024]{2,0,1:T(8,128)(2,1)}), bf16[8,8,1024]{2,0,1:T(8,128)(2,1)S(1)}, u32[]{:S(2)}, u32[]{:S(2)}) async-start(bf16[8,8,1024]{2,0,1:T(8,128)(2,1)} %bitcast.1), calls=%async_computation | async-start | bytes 262144 | tf_op jit(solution)/shard_map/all_to_all | solution.py:24
  131.8 159.8 %reduce-scatter.2.cloned.1.call-start = ((), (), s32[]{:S(2)}) async-start(), calls=%async_computation.3 | async-start | bytes 2064384 | tf_op jit(solution)/shard_map/reduce_scatter | solution.py:31
  206.8 84.7 %copy-start = (bf16[8,7168]{1,0:T(8,128)(2,1)S(1)}, bf16[8,7168]{1,0:T(8,128)(2,1)}, u32[]{:S(2)}) copy-start(bf16[8,7168]{1,0:T(8,128)(2,1)} %param.11) | copy-start | bytes 344068
Sparse Core Ops, SparseCore 0:
  10.2 68.9 all-gather.1
  224.4 67.0 reduce-scatter.1
where the time goes:
time: 307 us; the launch traced here: 306 us
  waiting for transfers between devices  130 us (42%)
  matrix products  64.8 us (21%)
  blocking collectives  55.7 us (18%)
  other arithmetic  37.4 us (12%)
  between operations  14.1 us (5%)
  starting transfers between devices  3.46 us (1%)
    reduce_scatter x1, waiting for transfers between devices, per_device(): lax.psum_scatter(total, 'row', scatter_dimension=0, tiled=True)  67.2 us
    all_gather x1, waiting for transfers between devices, per_device(): lax.all_gather(query_grads, 'row', axis=0, tiled=True)  62.4 us
    dot_general x3, matrix products, per_device(): jnp.dot(train_local, ritz_mats[which], precision=highest)  51.1 us
    psum x1, blocking collectives, per_device(): coeffs = lax.psum(local_terms, ('row', 'col'))  40.7 us
    reduce_sum x1, other arithmetic, per_device(): local_terms = jnp.sum(ritz_mats * grad_tile[None], axis=(1, 2))  35.5 us
    dot_general x1, matrix products, per_device(): lax.dot_general(acts_all, lax.all_gather(query_grads, 'row', axis=0, tile...  13.7 us
    all_gather x1, blocking collectives, per_device(): acts_all = lax.all_gather(query_acts, 'col', axis=0, tiled=True)  8.86 us
    psum x1, blocking collectives, per_device(): scores = lax.psum(score_terms, 'col')  6.17 us
  transfers between devices with their start and end apart: 3, of which 2 were waited for; matrix products, arithmetic and copies ran while one was open for 0% of the time, Pallas kernels for 0%

commit v1 on v0

--- a/solution.py
+++ b/solution.py
@@ -19,7 +19,8 @@
         preferred_element_type=jnp.float32,
     )
     local_terms = jnp.sum(ritz_mats * grad_tile[None], axis=(1, 2))
-    coeffs = lax.psum(local_terms, ("row", "col"))
+    inner = lax.psum(local_terms, "row")
+    coeffs = lax.psum(inner, "col")
     weights = coeffs / (eigenvalues * math.sqrt(QUERY * D_OUT))
     train_local = lax.all_to_all(train_acts, "row", split_axis=1, concat_axis=0, tiled=True).astype(
         jnp.float32

time: 307 us -> 293 us (0.954)
  blocking collectives: 55.7 us -> 40.3 us
    psum x1 -> x2, blocking collectives: 40.7 us -> 25.3 us  [the longest x1 19.2 us: per_device(): inner = lax.psum(local_terms, 'row')]
  transfers between devices with their start and end apart: 3 -> 3, of which waited for: 2 -> 3; matrix products, arithmetic and copies ran while one was open for 0% -> 0% of each run, Pallas kernels for 0% -> 0%
where the time goes in v1:
time: 293 us; the launch traced here: 292 us
  waiting for transfers between devices  132 us (45%)
  matrix products  64.8 us (22%)
  blocking collectives  40.3 us (14%)
  other arithmetic  37.4 us (13%)
  between operations  14.1 us (5%)
  starting transfers between devices  3.45 us (1%)
    reduce_scatter x1, waiting for transfers between devices, per_device(): lax.psum_scatter(total, 'row', scatter_dimension=0, tiled=True)  68.1 us
    all_gather x1, waiting for transfers between devices, per_device(): lax.all_gather(query_grads, 'row', axis=0, tiled=True)  62.4 us
    dot_general x3, matrix products, per_device(): jnp.dot(train_local, ritz_mats[which], precision=highest)  51.1 us
    reduce_sum x1, other arithmetic, per_device(): local_terms = jnp.sum(ritz_mats * grad_tile[None], axis=(1, 2))  35.5 us
    psum x1, blocking collectives, per_device(): inner = lax.psum(local_terms, 'row')  19.2 us
    dot_general x1, matrix products, per_device(): lax.dot_general(acts_all, lax.all_gather(query_grads, 'row', axis=0, tile...  13.7 us
    all_gather x1, blocking collectives, per_device(): acts_all = lax.all_gather(query_acts, 'col', axis=0, tiled=True)  8.86 us
    psum x1, blocking collectives, per_device(): scores = lax.psum(score_terms, 'col')  6.17 us
  transfers between devices with their start and end apart: 3, of which 3 were waited for; matrix products, arithmetic and copies ran while one was open for 0% of the time, Pallas kernels for 0%

profile of v1, /device:TPU:0, one launch (start us, length us, event | category | flops | bytes accessed | tf_op | source)
XLA Modules:
  0.0 292.3 jit_solution(13096004694386192556)
XLA Ops:
  7.2 0.0 all-gather.2.cloned.1.call-start
  7.2 0.7 all-gather.2.cloned.1.call-update
  7.9 8.9 %all_gather.6 = bf16[256,1024]{1,0:T(8,128)(2,1)S(1)} all-gather(bf16[64,1024]{1,0:T(8,128)(2,1)} %param.6), channel_id=1, replica_groups=mesh['row'=8,'col'=4] {'col'}, dimensions={0}, use_global_device_ids=true | all-gather | bytes 655360 | tf_op jit(solution)/shard_map/all_gather | solution.py:14
  16.8 62.4 %all-gather.2.cloned.1.call-done = bf16[256,7168]{1,0:T(8,128)(2,1)} async-done(((bf16[32,7168]{1,0:T(8,128)(2,1)}), bf16[256,7168]{1,0:T(8,128)(2,1)}) %all-gather.2.cloned.1.call-update) | async-done | bytes 3670032 | tf_op jit(solution)/shard_map/all_gather | solution.py:17
  79.1 13.7 %fusion.28 = f32[1024,7168]{1,0:T(8,128)} fusion(bf16[256,1024]{1,0:T(8,128)(2,1)S(1)} %all_gather.6, bf16[256,7168]{1,0:T(8,128)(2,1)} %all-gather.2.cloned.1.call-done), kind=kOutput, calls=%fused_computation.22 | convolution fusion | flops 3758096384 | bytes 33554432 | tf_op jit(solution)/shard_map/dot_general | solution.py:15
  92.8 0.0 copy-start.1
  92.8 35.5 %multiply_reduce_fusion = f32[3]{0:T(128)S(1)} fusion(f32[3,1024,7168]{2,1,0:T(8,128)} %param.8, f32[1024,7168]{1,0:T(8,128)} %fusion.28), kind=kLoop, calls=%fused_computation | loop fusion | flops 44040188 | bytes 117440528 | tf_op jit(solution)/shard_map/reduce_sum | solution.py:21
  128.4 19.2 %psum.21 = f32[3]{0:T(128)S(1)} all-reduce(f32[3]{0:T(128)S(1)} %multiply_reduce_fusion), channel_id=1, replica_groups=mesh['row'=8,'col'=4] {'row'}, use_global_device_ids=true, to_apply=%region_1.0 | all-reduce | flops 3 | bytes 24 | tf_op jit(solution)/shard_map/psum | solution.py:22
  147.5 3.4 %all-to-all-start = ((bf16[8,8,1024]{2,0,1:T(8,128)(2,1)}), bf16[8,8,1024]{2,0,1:T(8,128)(2,1)S(1)}, u32[]{:S(2)}, u32[]{:S(2)}) async-start(bf16[8,8,1024]{2,0,1:T(8,128)(2,1)} %bitcast.1), calls=%async_computation | async-start | bytes 262144 | tf_op jit(solution)/shard_map/all_to_all | solution.py:25
  150.9 0.0 reduce-scatter.2.cloned.1.call-start
  151.0 6.1 %psum.22 = f32[3]{0:T(128)S(1)} all-reduce(f32[3]{0:T(128)S(1)} %psum.21), channel_id=1, replica_groups=mesh['row'=8,'col'=4] {'col'}, use_global_device_ids=true, to_apply=%region_2.0 | all-reduce | flops 3 | bytes 24 | tf_op jit(solution)/shard_map/psum | solution.py:23
  157.1 0.0 copy-done.1
  157.1 0.7 fusion.27
  157.8 0.4 all-to-all-done
  158.2 15.6 %fusion.15 = f32[64,7168]{1,0:T(8,128)S(1)} fusion(f32[3,1024,7168]{2,1,0:T(8,128)} %param.8, f32[]{:T(128)} %bitcast.5, bf16[8,8,1024]{2,0,1:T(8,128)(2,1)S(1)} %all-to-all-done), kind=kOutput, calls=%fused_computation.12 | convolution fusion | flops 5637603328 | bytes 31326720 | tf_op jit(solution)/shard_map/dot_general | solution.py:31
  173.8 18.0 %fusion.12 = f32[64,7168]{1,0:T(8,128)S(1)} fusion(f32[64,7168]{1,0:T(8,128)S(1)} %fusion.15, f32[3,1024,7168]{2,1,0:T(8,128)} %param.8, f32[]{:T(128)} %bitcast, bf16[8,8,1024]{2,0,1:T(8,128)(2,1)S(1)} %all-to-all-done), kind=kOutput, calls=%fused_computation.11 | convolution fusion | flops 5638062080 | bytes 33161728 | tf_op jit(solution)/shard_map/dot_general | solution.py:31
  191.8 0.0 copy-start
  191.8 17.5 %fusion.21 = f32[64,7168]{1,0:T(8,128)} fusion(f32[64,7168]{1,0:T(8,128)S(1)} %fusion.12, f32[3,1024,7168]{2,1,0:T(8,128)} %param.8, f32[]{:T(128)} %bitcast.8, bf16[8,8,1024]{2,0,1:T(8,128)(2,1)S(1)} %all-to-all-done), kind=kOutput, calls=%fused_computation.14 | convolution fusion | flops 5638062080 | bytes 33161728 | tf_op jit(solution)/shard_map/dot_general | solution.py:31
  209.3 0.0 reduce-scatter.2.cloned.1.call-update
  209.3 68.1 %reduce-scatter.2.cloned.1.call-done = f32[8,7168]{1,0:T(8,128)} async-done(((f32[64,7168]{1,0:T(8,128)}), f32[8,7168]{1,0:T(8,128)}) %reduce-scatter.2.cloned.1.call-update) | async-done | bytes 229392 | tf_op jit(solution)/shard_map/reduce_scatter | solution.py:32
  277.5 0.0 copy-done
  277.5 1.8 multiply_reduce_fusion.1
  279.3 6.2 %psum.23 = f32[8]{0:T(128)} all-reduce(f32[8]{0:T(128)S(1)} %broadcast_multiply_fusion), channel_id=1, replica_groups=mesh['row'=8,'col'=4] {'col'}, use_global_device_ids=true, to_apply=%region_5.0 | all-reduce | flops 8 | bytes 64 | tf_op jit(solution)/shard_map/psum | solution.py:34
  (2 shorter events, 0.0 us)
Async XLA Ops:
  7.2 72.0 %all-gather.2.cloned.1.call-start = ((), (), s32[]{:S(2)}) async-start(), calls=%async_computation.2 | async-start | bytes 4128768 | tf_op jit(solution)/shard_map/all_gather | solution.py:17
  92.8 64.3 %copy-start.1 = (f32[3]{0:T(128)S(1)}, f32[3]{0:T(128)}, u32[]{:S(2)}) copy-start(f32[3]{0:T(128)} %param.9) | copy-start | bytes 40
  147.5 10.7 %all-to-all-start = ((bf16[8,8,1024]{2,0,1:T(8,128)(2,1)}), bf16[8,8,1024]{2,0,1:T(8,128)(2,1)S(1)}, u32[]{:S(2)}, u32[]{:S(2)}) async-start(bf16[8,8,1024]{2,0,1:T(8,128)(2,1)} %bitcast.1), calls=%async_computation | async-start | bytes 262144 | tf_op jit(solution)/shard_map/all_to_all | solution.py:25
  150.9 126.5 %reduce-scatter.2.cloned.1.call-start = ((), (), s32[]{:S(2)}) async-start(), calls=%async_computation.3 | async-start | bytes 2064384 | tf_op jit(solution)/shard_map/reduce_scatter | solution.py:32
  191.8 85.7 %copy-start = (bf16[8,7168]{1,0:T(8,128)(2,1)S(1)}, bf16[8,7168]{1,0:T(8,128)(2,1)}, u32[]{:S(2)}) copy-start(bf16[8,7168]{1,0:T(8,128)(2,1)} %param.11) | copy-start | bytes 344068
Sparse Core Ops, SparseCore 0:
  10.2 68.9 all-gather.1
  209.4 67.9 reduce-scatter.1
